TPU v7x, 32 devices: a whole 2x2x4 slice. The times are simulated.
32 devices in a mesh: rx: 16 (over z, y, core), shot: 2 (over x).
Axes of the slice: x: 2, y: 2, z: 4, core: 2. Of those that a mesh axis runs over, the one named last changes fastest.
Arguments:
- data: bfloat16 [3, 2, 4, 128, 128, 128], P(None, None, None, 'rx', 'shot'), may hold values from -6 to 6
- mixing: float32 [3, 2, 4, 4, 128, 128], P(None, None, None, None, 'rx'), may hold values from -3 to 3
- counts: int32 [3, 128], P(None, 'rx'), may hold values from 0 to 64
Outputs:
- fields: bfloat16 [3, 2, 4, 128, 128, 128], P(None, None, None, 'rx', 'shot')
- gram: float32 [3, 2, 128, 128, 128], P(None, None, 'rx', 'shot')
All inputs are finite; a program needn't handle non-finite values.
Results may differ from a plain program's by a relative error of at most 0.0091.
Values may be sent and summed in bfloat16 or wider, within the bound.
A program may use at most 128 MiB of HBM per device.

v0:
```python
import functools
import math

import jax
import jax.numpy as jnp
import numpy as np
from jax import lax
from jax.experimental import pallas as pl
from jax.experimental.pallas import tpu as pltpu
from jax.sharding import PartitionSpec as P

MESH = pl.DeviceIdType.MESH
NT = (((1,), (1,)), ((), ()))
TN = (((0,), (0,)), ((), ()))


def host_table(size, sign):
    steps = np.arange(size)
    angles = (steps[:, None] * steps[None, :] % size) * (2.0 * math.pi / size)
    factor = 1.0 / math.sqrt(size)
    cosine = np.cos(angles) * factor
    sine = np.sin(angles) * (factor * sign)
    table = np.stack(
        [np.stack([cosine, -sine], axis=1), np.stack([sine, cosine], axis=1)], axis=0
    )
    return table.astype(np.float32)


def flat(values):
    half = values.shape[0] * values.shape[1]
    return jnp.asarray(values.reshape(half, -1), jnp.bfloat16)


def tables(rx_size, ry_size, peers):
    lines = rx_size // peers
    ry_forward = host_table(ry_size, 1.0)
    rx_forward = host_table(rx_size, 1.0)
    rx_inverse = host_table(rx_size, -1.0)
    ry_inverse = host_table(ry_size, -1.0)
    first = flat(ry_forward.transpose(2, 3, 0, 1))
    split = rx_forward.reshape(2, peers, lines, 2, rx_size).transpose(1, 0, 2, 3, 4)
    second = jnp.asarray(split.reshape(2 * rx_size, 2 * rx_size), jnp.bfloat16)
    back = rx_inverse.transpose(2, 3, 0, 1)
    cut = back.reshape(2, peers, lines, 2, rx_size).transpose(1, 0, 2, 3, 4)
    third = jnp.asarray(cut.reshape(2 * rx_size, 2 * rx_size), jnp.bfloat16)
    whole = flat(back)
    fourth = flat(ry_inverse)
    return first, second, third, whole, fourth


def dot(left, right, dims):
    return lax.dot_general(left, right, dims, preferred_element_type=jnp.float32)


def kernel(
    peers, groups,
    data_ref, mixing_ref, passing_ref, t1, t2, t3, tg, t4,
    fields_ref, gram_ref,
    send1, recv1, send2, recv2, gbuf, stage, lift,
    out1_sem, in1_sem, out2_sem, in2_sem, gout_sem, gin_sem,
):
    bins, _, comps, lines, shots, ry_size = data_ref.shape
    waves = mixing_ref.shape[4]
    rx_size = mixing_ref.shape[5]
    pairs = comps // 2
    rows = 2 * lines
    me = lax.axis_index("rx")
    group = lax.axis_index("shot")
    others = sorted(range(1, peers), key=lambda o: abs(o - peers // 2))

    barrier = pltpu.get_barrier_semaphore()
    for offset in others:
        pl.semaphore_signal(
            barrier, inc=1, device_id=(lax.rem(me + offset, peers), group), device_id_type=MESH
        )
    for offset in range(1, groups):
        pl.semaphore_signal(
            barrier, inc=1, device_id=(me, lax.rem(group + offset, groups)), device_id_type=MESH
        )

    def forward_y(f, mp):
        def line(l, carry):
            parts = [
                jnp.concatenate(
                    [data_ref[f, c, 2 * mp, l], data_ref[f, c, 2 * mp + 1, l]], axis=0
                )
                for c in range(2)
            ]
            out = dot(t1[...], jnp.concatenate(parts, axis=1), NT)
            for d in range(2):
                stage[pl.ds(d * lines + l, ry_size, stride=rows), :] = out[
                    d * ry_size : (d + 1) * ry_size
                ]
            return carry

        for l in range(lines):
            line(l, 0)

        def pack(p, carry):
            size = waves * rows
            block = stage[pl.ds(pl.multiple_of(p * size, size), size), :]
            send1[f, mp, p] = block.reshape(waves, rows, 2 * shots).astype(jnp.bfloat16)
            return carry

        lax.fori_loop(0, peers, pack, 0)
        recv1[f, mp, me] = send1[f, mp, me]

    def send(source, target, f, mp, out_sem, in_sem):
        for offset in others:
            to = lax.rem(me + offset, peers)
            pltpu.make_async_remote_copy(
                src_ref=source.at[f, mp, to],
                dst_ref=target.at[f, mp, me],
                send_sem=out_sem.at[f, mp],
                recv_sem=in_sem.at[f, mp],
                device_id=(to, group),
                device_id_type=MESH,
            ).start()

    def await_all(buffer, f, mp, sem):
        part = buffer.at[f, mp, pl.ds(0, peers - 1)]
        pltpu.make_async_copy(part, part, sem.at[f, mp]).wait()

    def middle(f):
        def step(kp, carry):
            downs = []
            for k2 in range(2):
                k = 2 * kp + k2
                real, imag = [], []
                for mp in range(pairs):
                    seen = recv1[f, mp, :, k].reshape(2 * rx_size, 2 * shots)
                    ks = dot(seen, t2[...], TN)
                    for m2 in range(2):
                        real.append(ks[m2 * shots : (m2 + 1) * shots, :rx_size])
                        imag.append(ks[m2 * shots : (m2 + 1) * shots, rx_size:])
                mask = passing_ref[f, pl.ds(k, 1), :]
                mixed = []
                for o in range(comps):
                    total_r, total_i = None, None
                    for i in range(comps):
                        ar = mixing_ref[f, 0, o, i, pl.ds(k, 1), :]
                        ai = mixing_ref[f, 1, o, i, pl.ds(k, 1), :]
                        term_r = ar * real[i] - ai * imag[i]
                        term_i = ar * imag[i] + ai * real[i]
                        total_r = term_r if i == 0 else total_r + term_r
                        total_i = term_i if i == 0 else total_i + term_i
                    mixed.append(
                        jnp.concatenate([total_r * mask, total_i * mask], axis=1).astype(jnp.bfloat16)
                    )
                downs.append(mixed[1])
                for mp in range(pairs):
                    side = jnp.concatenate([mixed[2 * mp], mixed[2 * mp + 1]], axis=0)
                    out = dot(t3[...], side, NT).astype(jnp.bfloat16)
                    send2[f, mp, :, k] = out.reshape(peers, rows, 2 * shots)
            down = dot(tg[...], jnp.concatenate(downs, axis=0), NT)
            gbuf[group, f, kp] = down.astype(jnp.bfloat16)
            return carry

        lax.fori_loop(0, waves // 2, step, 0)
        for mp in range(pairs):
            recv2[f, mp, me] = send2[f, mp, me]

    def gram_send(f):
        for offset in range(1, groups):
            pltpu.make_async_remote_copy(
                src_ref=gbuf.at[group, f],
                dst_ref=gbuf.at[group, f],
                send_sem=gout_sem.at[f, offset],
                recv_sem=gin_sem.at[f, offset],
                device_id=(me, lax.rem(group + offset, groups)),
                device_id_type=MESH,
            ).start()

    def gram_wait(f):
        for offset in range(1, groups):
            part = gbuf.at[lax.rem(group + groups - offset, groups), f]
            pltpu.make_async_copy(part, part, gin_sem.at[f, offset]).wait()

    def gram(f):
        count = rx_size // groups
        first = pl.multiple_of(group * count, count)
        weight = 1.0 / (shots * groups)

        def step(kp, carry):
            for k2 in range(2):
                lanes = slice(k2 * shots, (k2 + 1) * shots)

                def take(start, size):
                    return jnp.concatenate(
                        [gbuf[j, f, kp, pl.ds(start, size), :][:, lanes] for j in range(groups)], axis=1
                    )

                real, imag = take(0, rx_size), take(rx_size, rx_size)
                mine = jnp.concatenate([take(first, count), take(rx_size + first, count)], axis=0)
                by_real, by_imag = dot(mine, real, NT), dot(mine, imag, NT)
                gram_ref[f, 0, 2 * kp + k2] = (by_real[:count] + by_imag[count:]) * weight
                gram_ref[f, 1, 2 * kp + k2] = (by_real[count:] - by_imag[:count]) * weight
            return carry

        lax.fori_loop(0, waves // 2, step, 0)

    def inverse_y(f, mp):
        def unpack(p, carry):
            size = waves * rows
            lift[pl.ds(pl.multiple_of(p * size, size), size), :] = (
                recv2[f, mp, p].reshape(size, 2 * shots).astype(jnp.float32)
            )
            return carry

        lax.fori_loop(0, peers, unpack, 0)
        for l in range(lines):
            left = jnp.concatenate(
                [lift[pl.ds(c * lines + l, ry_size, stride=rows), :] for c in range(2)], axis=0
            ).astype(jnp.bfloat16)
            out = dot(left, t4[...], TN).astype(jnp.bfloat16)
            for m2 in range(2):
                for d in range(2):
                    fields_ref[f, d, 2 * mp + m2, l] = out[
                        m2 * shots : (m2 + 1) * shots, d * ry_size : (d + 1) * ry_size
                    ]

    for f in range(bins):
        for mp in range(pairs):
            forward_y(f, mp)
            if f == 0 and mp == 0:
                pl.semaphore_wait(barrier, peers - 1 + groups - 1)
            send(send1, recv1, f, mp, out1_sem, in1_sem)
    for f in range(bins):
        for mp in range(pairs):
            await_all(recv1, f, mp, in1_sem)
        middle(f)
        for mp in range(pairs):
            send(send2, recv2, f, mp, out2_sem, in2_sem)
        gram_send(f)
        if f > 0:
            gram_wait(f - 1)
            gram(f - 1)
    gram_wait(bins - 1)
    gram(bins - 1)
    for f in range(bins):
        for mp in range(pairs):
            await_all(recv2, f, mp, in2_sem)
            inverse_y(f, mp)
    for f in range(bins):
        for mp in range(pairs):
            await_all(send1, f, mp, out1_sem)
            await_all(send2, f, mp, out2_sem)
        for offset in range(1, groups):
            part = gbuf.at[group, f]
            pltpu.make_async_copy(part, part, gout_sem.at[f, offset]).wait()


def fused(peers, groups, data, mixing, counts):
    bins, _, comps, lines, shots, ry_size = data.shape
    waves, rx_size = mixing.shape[4:]
    pairs = comps // 2
    wave_index = jnp.arange(rx_size, dtype=jnp.int32)
    radial = jnp.minimum(wave_index, rx_size - wave_index)
    passing = (radial[None, None, :] <= counts[:, :, None]).astype(jnp.float32)
    blocks = (bins, pairs, peers, waves, 2 * lines, 2 * shots)
    dma = pltpu.SemaphoreType.DMA
    vmem = pl.BlockSpec(memory_space=pltpu.VMEM)
    return pl.pallas_call(
        functools.partial(kernel, peers, groups),
        out_shape=(
            jax.ShapeDtypeStruct(data.shape, jnp.bfloat16),
            jax.ShapeDtypeStruct((bins, 2, waves, rx_size // groups, rx_size), jnp.float32),
        ),
        in_specs=[vmem] * 8,
        out_specs=(vmem, vmem),
        scratch_shapes=[pltpu.VMEM(blocks, jnp.bfloat16)] * 4
        + [
            pltpu.VMEM((groups, bins, waves // 2, 2 * rx_size, 2 * shots), jnp.bfloat16),
            pltpu.VMEM((ry_size * 2 * lines, 2 * shots), jnp.float32),
            pltpu.VMEM((ry_size * 2 * lines, 2 * shots), jnp.float32),
            dma((bins, pairs)), dma((bins, pairs)), dma((bins, pairs)), dma((bins, pairs)),
            dma((bins, groups)), dma((bins, groups)),
        ],
        compiler_params=pltpu.CompilerParams(
            collective_id=0, has_side_effects=True, vmem_limit_bytes=60 * 1024 * 1024
        ),
    )(data, mixing, passing, *tables(rx_size, ry_size, peers))


def dft_table(size, sign):
    steps = jnp.arange(size, dtype=jnp.int32)
    phases = steps[:, None] * steps[None, :] % size
    angles = phases.astype(jnp.float32) * (2.0 * math.pi / size)
    factor = 1.0 / math.sqrt(size)
    cosine = jnp.cos(angles) * factor
    sine = jnp.sin(angles) * (factor * sign)
    top_rows = jnp.stack([cosine, -sine], axis=1)
    low_rows = jnp.stack([sine, cosine], axis=1)
    return jnp.stack([top_rows, low_rows], axis=0).astype(jnp.bfloat16)


def apply_mix(matrix, values):
    return jnp.einsum("foikq,fikqs->fokqs", matrix, values, precision=lax.Precision.HIGHEST)


def per_device(data, mixing, counts):
    rx_size = mixing.shape[5]
    ry_size = data.shape[5]
    shots_here = data.shape[4]
    bin_count = data.shape[0]
    ry_forward = dft_table(ry_size, 1.0)
    rx_forward = dft_table(rx_size, 1.0)
    rx_inverse = dft_table(rx_size, -1.0)
    ry_inverse = dft_table(ry_size, -1.0)
    spectra = jnp.einsum(
        "fcmlsy,cydk->fdmkls", data, ry_forward, preferred_element_type=jnp.float32
    ).astype(jnp.bfloat16)
    pencils = jnp.stack(
        [
            lax.all_to_all(spectra[number], "rx", split_axis=2, concat_axis=3, tiled=True)
            for number in range(bin_count)
        ],
        axis=0,
    )
    kspace = jnp.einsum(
        "fcmkxs,cxdq->fdmkqs", pencils, rx_forward, preferred_element_type=jnp.float32
    )
    wave_index = jnp.arange(rx_size, dtype=jnp.int32)
    radial = jnp.minimum(wave_index, rx_size - wave_index)
    passing = (radial[None, None, :] <= counts[:, :, None]).astype(jnp.float32)
    mixed_real = apply_mix(mixing[:, 0], kspace[:, 0]) - apply_mix(mixing[:, 1], kspace[:, 1])
    mixed_imag = apply_mix(mixing[:, 0], kspace[:, 1]) + apply_mix(mixing[:, 1], kspace[:, 0])
    mixed = (
        jnp.stack([mixed_real, mixed_imag], axis=1) * passing[:, None, None, :, :, None]
    ).astype(jnp.bfloat16)
    spaced = jnp.einsum(
        "fcmkqs,cqdx->fdmkxs", mixed, rx_inverse, preferred_element_type=jnp.float32
    ).astype(jnp.bfloat16)
    downgo = spaced[:, :, 1]
    weight = 1.0 / (shots_here * lax.axis_size("shot"))
    row_count = rx_size // lax.axis_size("shot")
    first_row = lax.axis_index("shot") * row_count
    piece = lax.all_gather(downgo, "shot", axis=4, tiled=True)
    product = jnp.einsum(
        "fckxs,fdkzs->xfcdkz",
        lax.dynamic_slice_in_dim(piece, first_row, row_count, 3),
        piece,
        preferred_element_type=jnp.float32,
    )
    gram_rows = (
        jnp.stack(
            [product[:, :, 0, 0] + product[:, :, 1, 1], product[:, :, 1, 0] - product[:, :, 0, 1]],
            axis=2,
        )
        * weight
    )
    gram = jnp.transpose(gram_rows, (1, 2, 3, 0, 4))
    returned = jnp.stack(
        [
            lax.all_to_all(spaced[number], "rx", split_axis=3, concat_axis=2, tiled=True)
            for number in range(bin_count)
        ],
        axis=0,
    )
    fields = jnp.einsum(
        "fcmkls,ckdy->fdmlsy", returned, ry_inverse, preferred_element_type=jnp.float32
    ).astype(jnp.bfloat16)
    return (fields, gram)


def solution(mesh):
    peers, groups = mesh.shape["rx"], mesh.shape["shot"]

    def device_part(data, mixing, counts):
        _, _, comps, lines, shots, _ = data.shape
        waves = mixing.shape[4]
        if lines % 8 == 0 and shots % 64 == 0 and waves % 2 == 0 and comps % 2 == 0:
            return fused(peers, groups, data, mixing, counts)
        return per_device(data, mixing, counts)

    placed = (
        P(None, None, None, "rx", "shot", None),
        P(None, None, None, None, "rx", None),
        P(None, "rx"),
    )
    return jax.shard_map(
        device_part,
        mesh=mesh,
        in_specs=placed,
        out_specs=(P(None, None, None, "rx", "shot", None), P(None, None, "rx", "shot", None)),
        check_vma=False,
    )
```

profile of v0, /device:TPU:0, one launch (start us, length us, event | category | flops | bytes accessed | tf_op | source)
XLA Modules:
  0.0 153.6 jit_solution(3833236515020132067)
XLA Ops:
  0.6 1.4 compare_convert_fusion.passing_ref
  2.0 145.8 %shard_map.95 = (bf16[3,2,4,8,64,128]{5,4,3,2,1,0:T(8,128)(2,1)}, f32[3,2,8,64,128]{4,3,2,1,0:T(8,128)}) custom-call(bf16[3,2,4,8,64,128]{5,4,3,2,1,0:T(8,128)(2,1)} %data_ref.1, f32[3,2,4,4,8,128]{5,4,3,2,1,0:T(8,128)} %mixing_ref.1, f32[3,8,128]{2,1,0:T(8,128)} %compare_convert_fusion.passing_ref, bf16[256,256]{1,0:T(8,128)(2,1)} %constant.8.clone.t1.t4, ...), custom_call_target="tpu_custom_call" | custom-call | tf_op jit(solution)/shard_map/pallas_call | solution.py:263
  147.8 0.0 copy-start
  147.8 4.7 %copy.12 = bf16[3,2,4,8,64,128]{5,4,3,2,1,0:T(8,128)(2,1)} copy(bf16[3,2,4,8,64,128]{5,4,3,2,1,0:T(8,128)(2,1)} %get-tuple-element.4) | data formatting | bytes 6291456
  152.5 0.0 copy-done
  152.5 1.1 copy.13
  (1 shorter events, 0.0 us)
Async XLA Ops:
  147.8 4.7 %copy-start = (f32[3,2,8,64,128]{4,3,2,1,0:T(8,128)S(1)}, f32[3,2,8,64,128]{4,3,2,1,0:T(8,128)}, u32[]{:S(2)}) copy-start(f32[3,2,8,64,128]{4,3,2,1,0:T(8,128)} %get-tuple-element.5) | copy-start | bytes 4718596
where the time goes:
time: 154 us
  Pallas kernels  146 us (95%)
  local copies, waits for them, and re-layouts  5.85 us (4%)
    pallas_call x1, Pallas kernels, fused(): pl.pallas_call(functools.partial(kernel, peers, groups), out_shape=(jax.S...  146 us
    unnamed x4, local copies, waits for them, and re-layouts  5.85 us

commit v1 on v0

--- a/solution.py
+++ b/solution.py
@@ -54,10 +54,11 @@
 
 def kernel(
     peers, groups,
-    data_ref, mixing_ref, passing_ref, t1, t2, t3, tg, t4,
+    counts_ref, data_hbm, mixing_hbm, t1_hbm, t2_hbm, t3_hbm, tg_hbm, t4_hbm,
     fields_ref, gram_ref,
+    data_ref, mixing_ref, t1, t2, t3, tg, t4,
     send1, recv1, send2, recv2, gbuf, stage, lift,
-    out1_sem, in1_sem, out2_sem, in2_sem, gout_sem, gin_sem,
+    out1_sem, in1_sem, out2_sem, in2_sem, gout_sem, gin_sem, load_sem, data_sem,
 ):
     bins, _, comps, lines, shots, ry_size = data_ref.shape
     waves = mixing_ref.shape[4]
@@ -68,6 +69,19 @@
     group = lax.axis_index("shot")
     others = sorted(range(1, peers), key=lambda o: abs(o - peers // 2))
 
+    def load_data(f, mp):
+        span = (f, slice(None), pl.ds(2 * mp, 2))
+        return pltpu.make_async_copy(data_hbm.at[span], data_ref.at[span], data_sem.at[f, mp])
+
+    loads = [
+        pltpu.make_async_copy(source, target, load_sem.at[number])
+        for number, (source, target) in enumerate(
+            [(t1_hbm, t1), (t2_hbm, t2), (t3_hbm, t3), (tg_hbm, tg), (t4_hbm, t4), (mixing_hbm, mixing_ref)]
+        )
+    ]
+    load_data(0, 0).start()
+    loads[0].start()
+
     barrier = pltpu.get_barrier_semaphore()
     for offset in others:
         pl.semaphore_signal(
@@ -77,6 +91,15 @@
         pl.semaphore_signal(
             barrier, inc=1, device_id=(me, lax.rem(group + offset, groups)), device_id_type=MESH
         )
+
+    for f in range(bins):
+        for mp in range(pairs):
+            if f + mp > 0:
+                load_data(f, mp).start()
+    for load in loads[1:]:
+        load.start()
+    wave_index = lax.broadcasted_iota(jnp.int32, (1, rx_size), 1)
+    radial = jnp.minimum(wave_index, rx_size - wave_index)
 
     def forward_y(f, mp):
         def line(l, carry):
@@ -96,26 +119,29 @@
         for l in range(lines):
             line(l, 0)
 
-        def pack(p, carry):
-            size = waves * rows
+        if f == 0 and mp == 0:
+            pl.semaphore_wait(barrier, peers - 1 + groups - 1)
+        size = waves * rows
+
+        def packed(p):
             block = stage[pl.ds(pl.multiple_of(p * size, size), size), :]
-            send1[f, mp, p] = block.reshape(waves, rows, 2 * shots).astype(jnp.bfloat16)
-            return carry
-
-        lax.fori_loop(0, peers, pack, 0)
-        recv1[f, mp, me] = send1[f, mp, me]
-
-    def send(source, target, f, mp, out_sem, in_sem):
+            return block.reshape(waves, rows, 2 * shots).astype(jnp.bfloat16)
+
         for offset in others:
             to = lax.rem(me + offset, peers)
-            pltpu.make_async_remote_copy(
-                src_ref=source.at[f, mp, to],
-                dst_ref=target.at[f, mp, me],
-                send_sem=out_sem.at[f, mp],
-                recv_sem=in_sem.at[f, mp],
-                device_id=(to, group),
-                device_id_type=MESH,
-            ).start()
+            send1[f, mp, to] = packed(to)
+            copy_to(send1, recv1, f, mp, out1_sem, in1_sem, to)
+        recv1[f, mp, me] = packed(me)
+
+    def copy_to(source, target, f, mp, out_sem, in_sem, to):
+        pltpu.make_async_remote_copy(
+            src_ref=source.at[f, mp, to],
+            dst_ref=target.at[f, mp, me],
+            send_sem=out_sem.at[f, mp],
+            recv_sem=in_sem.at[f, mp],
+            device_id=(to, group),
+            device_id_type=MESH,
+        ).start()
 
     def await_all(buffer, f, mp, sem):
         part = buffer.at[f, mp, pl.ds(0, peers - 1)]
@@ -133,7 +159,7 @@
                     for m2 in range(2):
                         real.append(ks[m2 * shots : (m2 + 1) * shots, :rx_size])
                         imag.append(ks[m2 * shots : (m2 + 1) * shots, rx_size:])
-                mask = passing_ref[f, pl.ds(k, 1), :]
+                mask = jnp.where(radial <= counts_ref[f, k], 1.0, 0.0)
                 mixed = []
                 for o in range(comps):
                     total_r, total_i = None, None
@@ -221,16 +247,19 @@
 
     for f in range(bins):
         for mp in range(pairs):
+            load_data(f, mp).wait()
+            if f == 0 and mp == 0:
+                loads[0].wait()
             forward_y(f, mp)
-            if f == 0 and mp == 0:
-                pl.semaphore_wait(barrier, peers - 1 + groups - 1)
-            send(send1, recv1, f, mp, out1_sem, in1_sem)
+    for load in loads[1:]:
+        load.wait()
     for f in range(bins):
         for mp in range(pairs):
             await_all(recv1, f, mp, in1_sem)
         middle(f)
         for mp in range(pairs):
-            send(send2, recv2, f, mp, out2_sem, in2_sem)
+            for offset in others:
+                copy_to(send2, recv2, f, mp, out2_sem, in2_sem, lax.rem(me + offset, peers))
         gram_send(f)
         if f > 0:
             gram_wait(f - 1)
@@ -254,32 +283,38 @@
     bins, _, comps, lines, shots, ry_size = data.shape
     waves, rx_size = mixing.shape[4:]
     pairs = comps // 2
-    wave_index = jnp.arange(rx_size, dtype=jnp.int32)
-    radial = jnp.minimum(wave_index, rx_size - wave_index)
-    passing = (radial[None, None, :] <= counts[:, :, None]).astype(jnp.float32)
     blocks = (bins, pairs, peers, waves, 2 * lines, 2 * shots)
     dma = pltpu.SemaphoreType.DMA
+    results = 2 * math.prod(data.shape) + 8 * bins * waves * rx_size * rx_size // groups
     vmem = pl.BlockSpec(memory_space=pltpu.VMEM)
+    hbm = pl.BlockSpec(memory_space=pltpu.HBM)
+    table = pltpu.VMEM((2 * rx_size, 2 * rx_size), jnp.bfloat16)
+    table_y = pltpu.VMEM((2 * ry_size, 2 * ry_size), jnp.bfloat16)
     return pl.pallas_call(
         functools.partial(kernel, peers, groups),
         out_shape=(
-            jax.ShapeDtypeStruct(data.shape, jnp.bfloat16),
-            jax.ShapeDtypeStruct((bins, 2, waves, rx_size // groups, rx_size), jnp.float32),
+            pltpu.VMEM(data.shape, jnp.bfloat16),
+            pltpu.VMEM((bins, 2, waves, rx_size // groups, rx_size), jnp.float32),
         ),
-        in_specs=[vmem] * 8,
+        in_specs=[pl.BlockSpec(memory_space=pltpu.SMEM)] + [hbm] * 7,
         out_specs=(vmem, vmem),
-        scratch_shapes=[pltpu.VMEM(blocks, jnp.bfloat16)] * 4
+        scratch_shapes=[
+            pltpu.VMEM(data.shape, jnp.bfloat16),
+            pltpu.VMEM(mixing.shape, jnp.float32),
+            table_y, table, table, table, table_y,
+        ]
+        + [pltpu.VMEM(blocks, jnp.bfloat16)] * 4
         + [
             pltpu.VMEM((groups, bins, waves // 2, 2 * rx_size, 2 * shots), jnp.bfloat16),
             pltpu.VMEM((ry_size * 2 * lines, 2 * shots), jnp.float32),
             pltpu.VMEM((ry_size * 2 * lines, 2 * shots), jnp.float32),
             dma((bins, pairs)), dma((bins, pairs)), dma((bins, pairs)), dma((bins, pairs)),
-            dma((bins, groups)), dma((bins, groups)),
+            dma((bins, groups)), dma((bins, groups)), dma((6,)), dma((bins, pairs)),
         ],
         compiler_params=pltpu.CompilerParams(
-            collective_id=0, has_side_effects=True, vmem_limit_bytes=60 * 1024 * 1024
+            collective_id=0, has_side_effects=True, vmem_limit_bytes=67043328 - results - 131072
         ),
-    )(data, mixing, passing, *tables(rx_size, ry_size, peers))
+    )(counts, data, mixing, *tables(rx_size, ry_size, peers))
 
 
 def dft_table(size, sign):

time: 154 us -> 146 us (0.948)
  Pallas kernels: 146 us -> 142 us
  local copies, waits for them, and re-layouts: 5.85 us -> 2.81 us
    pallas_call x1, Pallas kernels: 146 us -> 142 us  [fused(): pl.pallas_call(functools.partial(kernel, peers, groups), out_shape=(pltpu...]
    unnamed x4 -> x2, local copies, waits for them, and re-layouts: 5.85 us -> 2.81 us
where the time goes in v1:
time: 146 us
  Pallas kernels  142 us (97%)
  local copies, waits for them, and re-layouts  2.81 us (2%)
    pallas_call x1, Pallas kernels, fused(): pl.pallas_call(functools.partial(kernel, peers, groups), out_shape=(pltpu...  142 us

profile of v1, /device:TPU:0, one launch (start us, length us, event | category | flops | bytes accessed | tf_op | source)
XLA Modules:
  0.0 145.9 jit_solution(8593057845130398012)
XLA Ops:
  0.6 142.5 %shard_map.95 = (bf16[3,2,4,8,64,128]{5,4,3,2,1,0:T(8,128)(2,1)S(1)}, f32[3,2,8,64,128]{4,3,2,1,0:T(8,128)S(1)}) custom-call(s32[3,8]{1,0:T(4,128)} %counts_ref.1, bf16[3,2,4,8,64,128]{5,4,3,2,1,0:T(8,128)(2,1)} %data_hbm.1, f32[3,2,4,4,8,128]{5,4,3,2,1,0:T(8,128)} %mixing_hbm.1, bf16[256,256]{1,0:T(8,128)(2,1)} %constant.6.clone.t1_hbm.t4_hbm, ...), custom_call_target="tpu_custom_call" | custom-call | tf_op jit(solution)/shard_map/pallas_call | solution.py:293
  143.1 1.7 %copy.12 = bf16[3,2,4,8,64,128]{5,4,3,2,1,0:T(8,128)(2,1)} copy(bf16[3,2,4,8,64,128]{5,4,3,2,1,0:T(8,128)(2,1)S(1)} %get-tuple-element.2) | data formatting | bytes 6291456
  144.8 1.1 copy.13

commit v2 on v1

--- a/solution.py
+++ b/solution.py
@@ -52,10 +52,56 @@
     return lax.dot_general(left, right, dims, preferred_element_type=jnp.float32)
 
 
+def inverse_y(peers, seen, lift, table, put):
+    _, waves, rows, lanes = seen.shape
+    lines, shots, ry_size = rows // 2, lanes // 2, peers * waves
+    size = waves * rows
+
+    def unpack(p, carry):
+        lift[pl.ds(pl.multiple_of(p * size, size), size), :] = (
+            seen[p].reshape(size, lanes).astype(jnp.float32)
+        )
+        return carry
+
+    lax.fori_loop(0, peers, unpack, 0)
+    for l in range(lines):
+        left = jnp.concatenate(
+            [lift[pl.ds(c * lines + l, ry_size, stride=rows), :] for c in range(2)], axis=0
+        ).astype(jnp.bfloat16)
+        out = dot(left, table[...], TN).astype(jnp.bfloat16)
+        for m2 in range(2):
+            for d in range(2):
+                put(d, m2, l, out[m2 * shots : (m2 + 1) * shots, d * ry_size : (d + 1) * ry_size])
+
+
+def finish(peers, fields_ref, gram_ref, last_ref, t4, out_fields, out_gram, lift, tail, sem):
+    bins, comps = fields_ref.shape[0], fields_ref.shape[2]
+    end = bins - 1
+    done = [pltpu.make_async_copy(gram_ref, out_gram, sem.at[bins])]
+    for f in range(bins):
+        span = (f,) if f < end else (f, slice(None), pl.ds(0, comps - 2))
+        done.append(pltpu.make_async_copy(fields_ref.at[span], out_fields.at[span], sem.at[f]))
+    for copy in done:
+        copy.start()
+
+    def put(d, m2, l, value):
+        tail[d, m2, l] = value
+
+    inverse_y(peers, last_ref, lift, t4, put)
+    done.append(
+        pltpu.make_async_copy(
+            tail, out_fields.at[end, :, pl.ds(comps - 2, 2)], sem.at[bins + 1]
+        )
+    )
+    done[-1].start()
+    for copy in done:
+        copy.wait()
+
+
 def kernel(
     peers, groups,
     counts_ref, data_hbm, mixing_hbm, t1_hbm, t2_hbm, t3_hbm, tg_hbm, t4_hbm,
-    fields_ref, gram_ref,
+    fields_ref, gram_ref, last_ref,
     data_ref, mixing_ref, t1, t2, t3, tg, t4,
     send1, recv1, send2, recv2, gbuf, stage, lift,
     out1_sem, in1_sem, out2_sem, in2_sem, gout_sem, gin_sem, load_sem, data_sem,
@@ -130,13 +176,13 @@
         for offset in others:
             to = lax.rem(me + offset, peers)
             send1[f, mp, to] = packed(to)
-            copy_to(send1, recv1, f, mp, out1_sem, in1_sem, to)
+            copy_to(send1, recv1.at[f, mp], f, mp, out1_sem, in1_sem, to)
         recv1[f, mp, me] = packed(me)
 
     def copy_to(source, target, f, mp, out_sem, in_sem, to):
         pltpu.make_async_remote_copy(
             src_ref=source.at[f, mp, to],
-            dst_ref=target.at[f, mp, me],
+            dst_ref=target.at[me],
             send_sem=out_sem.at[f, mp],
             recv_sem=in_sem.at[f, mp],
             device_id=(to, group),
@@ -184,7 +230,7 @@
 
         lax.fori_loop(0, waves // 2, step, 0)
         for mp in range(pairs):
-            recv2[f, mp, me] = send2[f, mp, me]
+            box2(f, mp)[me] = send2[f, mp, me]
 
     def gram_send(f):
         for offset in range(1, groups):
@@ -225,25 +271,8 @@
 
         lax.fori_loop(0, waves // 2, step, 0)
 
-    def inverse_y(f, mp):
-        def unpack(p, carry):
-            size = waves * rows
-            lift[pl.ds(pl.multiple_of(p * size, size), size), :] = (
-                recv2[f, mp, p].reshape(size, 2 * shots).astype(jnp.float32)
-            )
-            return carry
-
-        lax.fori_loop(0, peers, unpack, 0)
-        for l in range(lines):
-            left = jnp.concatenate(
-                [lift[pl.ds(c * lines + l, ry_size, stride=rows), :] for c in range(2)], axis=0
-            ).astype(jnp.bfloat16)
-            out = dot(left, t4[...], TN).astype(jnp.bfloat16)
-            for m2 in range(2):
-                for d in range(2):
-                    fields_ref[f, d, 2 * mp + m2, l] = out[
-                        m2 * shots : (m2 + 1) * shots, d * ry_size : (d + 1) * ry_size
-                    ]
+    def box2(f, mp):
+        return last_ref if (f, mp) == (bins - 1, pairs - 1) else recv2.at[f, mp]
 
     for f in range(bins):
         for mp in range(pairs):
@@ -259,7 +288,7 @@
         middle(f)
         for mp in range(pairs):
             for offset in others:
-                copy_to(send2, recv2, f, mp, out2_sem, in2_sem, lax.rem(me + offset, peers))
+                copy_to(send2, box2(f, mp), f, mp, out2_sem, in2_sem, lax.rem(me + offset, peers))
         gram_send(f)
         if f > 0:
             gram_wait(f - 1)
@@ -269,7 +298,12 @@
     for f in range(bins):
         for mp in range(pairs):
             await_all(recv2, f, mp, in2_sem)
-            inverse_y(f, mp)
+            if (f, mp) != (bins - 1, pairs - 1):
+
+                def put(d, m2, l, value):
+                    fields_ref[f, d, 2 * mp + m2, l] = value
+
+                inverse_y(peers, box2(f, mp), lift, t4, put)
     for f in range(bins):
         for mp in range(pairs):
             await_all(send1, f, mp, out1_sem)
@@ -285,19 +319,22 @@
     pairs = comps // 2
     blocks = (bins, pairs, peers, waves, 2 * lines, 2 * shots)
     dma = pltpu.SemaphoreType.DMA
-    results = 2 * math.prod(data.shape) + 8 * bins * waves * rx_size * rx_size // groups
+    gram_shape = (bins, 2, waves, rx_size // groups, rx_size)
+    results = 2 * math.prod(data.shape) + 4 * math.prod(gram_shape) + 2 * math.prod(blocks[2:])
     vmem = pl.BlockSpec(memory_space=pltpu.VMEM)
     hbm = pl.BlockSpec(memory_space=pltpu.HBM)
     table = pltpu.VMEM((2 * rx_size, 2 * rx_size), jnp.bfloat16)
     table_y = pltpu.VMEM((2 * ry_size, 2 * ry_size), jnp.bfloat16)
-    return pl.pallas_call(
+    all_tables = tables(rx_size, ry_size, peers)
+    fields, gram, last = pl.pallas_call(
         functools.partial(kernel, peers, groups),
         out_shape=(
             pltpu.VMEM(data.shape, jnp.bfloat16),
-            pltpu.VMEM((bins, 2, waves, rx_size // groups, rx_size), jnp.float32),
+            pltpu.VMEM(gram_shape, jnp.float32),
+            pltpu.VMEM(blocks[2:], jnp.bfloat16),
         ),
         in_specs=[pl.BlockSpec(memory_space=pltpu.SMEM)] + [hbm] * 7,
-        out_specs=(vmem, vmem),
+        out_specs=(vmem, vmem, vmem),
         scratch_shapes=[
             pltpu.VMEM(data.shape, jnp.bfloat16),
             pltpu.VMEM(mixing.shape, jnp.float32),
@@ -306,15 +343,31 @@
         + [pltpu.VMEM(blocks, jnp.bfloat16)] * 4
         + [
             pltpu.VMEM((groups, bins, waves // 2, 2 * rx_size, 2 * shots), jnp.bfloat16),
-            pltpu.VMEM((ry_size * 2 * lines, 2 * shots), jnp.float32),
-            pltpu.VMEM((ry_size * 2 * lines, 2 * shots), jnp.float32),
+            pltpu.VMEM(((ry_size + 1) * 2 * lines, 2 * shots), jnp.float32),
+            pltpu.VMEM(((ry_size + 1) * 2 * lines, 2 * shots), jnp.float32),
             dma((bins, pairs)), dma((bins, pairs)), dma((bins, pairs)), dma((bins, pairs)),
             dma((bins, groups)), dma((bins, groups)), dma((6,)), dma((bins, pairs)),
         ],
         compiler_params=pltpu.CompilerParams(
             collective_id=0, has_side_effects=True, vmem_limit_bytes=67043328 - results - 131072
         ),
-    )(counts, data, mixing, *tables(rx_size, ry_size, peers))
+    )(counts, data, mixing, *all_tables)
+    anywhere = pl.BlockSpec(memory_space=pl.ANY)
+    return pl.pallas_call(
+        functools.partial(finish, peers),
+        out_shape=(
+            jax.ShapeDtypeStruct(fields.shape, fields.dtype),
+            jax.ShapeDtypeStruct(gram.shape, gram.dtype),
+        ),
+        in_specs=[anywhere, anywhere, vmem, vmem],
+        out_specs=(hbm, hbm),
+        scratch_shapes=[
+            pltpu.VMEM(((ry_size + 1) * 2 * lines, 2 * shots), jnp.float32),
+            pltpu.VMEM((2, 2, lines, shots, ry_size), jnp.bfloat16),
+            dma((bins + 2,)),
+        ],
+        compiler_params=pltpu.CompilerParams(vmem_limit_bytes=8 * 1024 * 1024),
+    )(fields, gram, last, all_tables[4])
 
 
 def dft_table(size, sign):

time: 146 us -> 145 us (level)
  local copies, waits for them, and re-layouts: 2.81 us -> 0.01 us
  Pallas kernels: 142 us -> 144 us
    unnamed x2, local copies, waits for them, and re-layouts: 2.81 us -> 0.01 us
    pallas_call x0 -> x1, Pallas kernels: none -> 2.22 us  [fused(): pl.pallas_call(functools.partial(finish, peers), out_shape=(jax.ShapeDtyp...]
where the time goes in v2:
time: 145 us
  Pallas kernels  144 us (99%)
    pallas_call x1, Pallas kernels, fused(): pl.pallas_call(functools.partial(kernel, peers, groups), out_shape=(pltpu...  142 us

profile of v2, /device:TPU:0, one launch (start us, length us, event | category | flops | bytes accessed | tf_op | source)
XLA Modules:
  0.0 144.8 jit_solution(13020112705130678004)
XLA Ops:
  0.6 0.0 copy-start
  0.6 141.9 %shard_map.95 = (bf16[3,2,4,8,64,128]{5,4,3,2,1,0:T(8,128)(2,1)S(1)}, f32[3,2,8,64,128]{4,3,2,1,0:T(8,128)S(1)}, bf16[16,8,16,128]{3,2,1,0:T(8,128)(2,1)S(1)}) custom-call(s32[3,8]{1,0:T(4,128)} %counts_ref.1, bf16[3,2,4,8,64,128]{5,4,3,2,1,0:T(8,128)(2,1)} %data_hbm.1, f32[3,2,4,4,8,128]{5,4,3,2,1,0:T(8,128)} %mixing_hbm.1, ...), custom_call_target="tpu_custom_call" | custom-call | tf_op jit(solution)/shard_map/pallas_call | solution.py:329
  142.6 0.0 copy-done
  142.6 2.2 %shard_map.96 = (bf16[3,2,4,8,64,128]{5,4,3,2,1,0:T(8,128)(2,1)}, f32[3,2,8,64,128]{4,3,2,1,0:T(8,128)}) custom-call(bf16[3,2,4,8,64,128]{5,4,3,2,1,0:T(8,128)(2,1)S(1)} %get-tuple-element.5.fields_ref, f32[3,2,8,64,128]{4,3,2,1,0:T(8,128)S(1)} %get-tuple-element.6.gram_ref, bf16[16,8,16,128]{3,2,1,0:T(8,128)(2,1)S(1)} %get-tuple-element.7.last_ref, ...), custom_call_target="tpu_custom_call" | custom-call | tf_op jit(solution)/shard_map/pallas_call | solution.py:356
Async XLA Ops:
  0.6 142.0 %copy-start = (bf16[256,256]{1,0:T(8,128)(2,1)S(1)}, bf16[256,256]{1,0:T(8,128)(2,1)}, u32[]{:S(2)}) copy-start(bf16[256,256]{1,0:T(8,128)(2,1)} %constant.6.clone.t1_hbm.t4_hbm.t4) | copy-start | bytes 393220
